TPU v7x, 32 devices: a whole 2x2x4 slice. The times are simulated.
32 devices in a mesh: groups: 2 (over x), level: 16 (over z, y, core).
Axes of the slice: x: 2, y: 2, z: 4, core: 2. Of those that a mesh axis runs over, the one named last changes fastest.
Arguments:
- latents: bfloat16 [64, 256, 640], P(('groups', 'level')), parts along dimension 0, may hold values from -6 to 6
- levels: int32 [64], P(('groups', 'level')), parts along dimension 0, may hold values from 0 to 15
- back_reach: int32 [64], P(('groups', 'level')), parts along dimension 0, may hold values from 1 to 2
- text_ids: int32 [154], P('groups'), parts along dimension 0, may hold values from 0 to 49407
- text_table: bfloat16 [49408, 1024], P('level'), may hold values from -6 to 6
- text_proj: bfloat16 [1024, 640], replicated, may hold values from -0.75 to 0.75
- level_embed: float32 [16, 640], replicated, may hold values from -3 to 3
- step_rate: float32 [16], replicated, may hold values from 0.3 to 1
- norm_gain: float32 [640], replicated, may hold values from 0.5 to 1.5
- w_query: bfloat16 [640, 640], replicated
- w_key: bfloat16 [640, 640], replicated
- w_value: bfloat16 [640, 640], replicated, may hold values from -0.25 to 0.25
- w_out: bfloat16 [640, 640], replicated, may hold values from -0.25 to 0.25
Outputs:
- queue_out: bfloat16 [64, 256, 640], P(('groups', 'level')), parts along dimension 0
There are 2 independent parts, one for each index of `groups`. A program takes and returns all parts, laid end to end along the dimension named above; an argument that names none is the same for every part. Nothing has to cross between parts.
All inputs are finite; a program needn't handle non-finite values.
Results may differ from a plain program's by a relative error of at most 0.007.
Values may be sent and summed in bfloat16 or wider, within the bound.
A program may use at most 64 MiB of HBM per device.

v0:
```python
import jax
import jax.numpy as jnp
from jax import lax
from jax.sharding import PartitionSpec as P

DH = 64
BAND = 2
STEPS = 3


def extended(block, sides, width):
    for axis, dim in sides:
        count = lax.axis_size(axis)
        forward = [(i, i + 1) for i in range(count - 1)]
        forward.append((count - 1, 0))
        backward = [(target, source) for source, target in forward]
        low = lax.ppermute(
            lax.slice_in_dim(block, block.shape[dim] - width, None, axis=dim), axis, forward
        )
        high = lax.ppermute(lax.slice_in_dim(block, 0, width, axis=dim), axis, backward)
        block = jnp.concatenate([low, block, high], axis=dim)
    return block


def shifted_2(block, axis, distance):
    devices = range(lax.axis_size(axis))
    route = [((i - distance) % len(devices), i) for i in devices]
    return lax.ppermute(block, axis, route)


def per_device(
    latents,
    levels,
    back_reach,
    text_ids,
    text_table,
    text_proj,
    level_embed,
    step_rate,
    norm_gain,
    w_query,
    w_key,
    w_value,
    w_out,
):
    count = lax.axis_size("level")
    index = lax.axis_index("level")
    frames_dev, tokens, width = latents.shape
    heads = width // DH
    scale = 1.0 / DH**0.5
    total_frames = frames_dev * count
    vocab_rows = text_table.shape[0]
    one_text = (
        text_ids[:, None] == index * vocab_rows + jnp.arange(vocab_rows, dtype=jnp.int32)[None, :]
    ).astype(jnp.bfloat16)
    text_local = jnp.dot(one_text, text_table, preferred_element_type=jnp.float32)
    pooled = jnp.mean(lax.psum(text_local, "level"), axis=0)
    text_vec = jnp.dot(
        pooled.astype(jnp.bfloat16)[None, :], text_proj, preferred_element_type=jnp.float32
    )[0]
    level_count = level_embed.shape[0]

    def project(source, weight):
        flat = source.reshape(-1, width)
        return (
            jnp.dot(flat, weight, preferred_element_type=jnp.float32)
            .astype(jnp.bfloat16)
            .reshape(source.shape[0], tokens, heads, DH)
        )

    current = latents
    for step in range(STEPS):
        one_level = (levels[:, None] == jnp.arange(level_count, dtype=jnp.int32)[None, :]).astype(
            jnp.float32
        )
        cond = jnp.dot(one_level, level_embed, precision=lax.Precision.HIGHEST) + text_vec[None, :]
        rate = jnp.dot(one_level, step_rate[:, None], precision=lax.Precision.HIGHEST)[:, 0]
        hin = current.astype(jnp.float32) + cond[:, None, :]
        normed = (
            hin * lax.rsqrt(jnp.mean(hin * hin, axis=-1, keepdims=True) + 1e-06) * norm_gain
        ).astype(jnp.bfloat16)
        query = project(normed, w_query)
        paired = jnp.stack([project(normed, w_key), project(normed, w_value)])
        widened = extended(paired, (("level", 1),), BAND)
        keys = widened[0]
        values = widened[1]
        position = index * frames_dev + jnp.arange(frames_dev, dtype=jnp.int32)
        score_list = []
        valid_list = []
        for offset in range(-BAND, BAND + 1):
            shifted = keys[BAND + offset : BAND + offset + frames_dev]
            raw = (
                jnp.einsum("fphd,fphd->fph", query, shifted, preferred_element_type=jnp.float32)
                * scale
            )
            valid = (
                (offset >= -back_reach)
                & (position + offset >= 0)
                & (position + offset < total_frames)
            )
            score_list.append(jnp.where(valid[:, None, None], raw, -1e30))
            valid_list.append(valid.astype(jnp.float32)[:, None, None])
        scores = jnp.stack(score_list)
        masks = jnp.stack(valid_list)
        top = jnp.max(scores, axis=0)
        expo = jnp.exp(scores - top[None]) * masks
        weights = (expo / jnp.sum(expo, axis=0)[None]).astype(jnp.bfloat16)
        attended = jnp.zeros((frames_dev, tokens, heads, DH), jnp.float32)
        for slot, offset in enumerate(range(-BAND, BAND + 1)):
            shifted = values[BAND + offset : BAND + offset + frames_dev]
            attended = attended + weights[slot].astype(jnp.float32)[..., None] * shifted.astype(
                jnp.float32
            )
        attended = attended.astype(jnp.bfloat16).reshape(-1, width)
        noise_pred = jnp.dot(attended, w_out, preferred_element_type=jnp.float32).reshape(
            frames_dev, tokens, width
        )
        current = (current.astype(jnp.float32) - rate[:, None, None] * noise_pred).astype(
            jnp.bfloat16
        )
        current = shifted_2(current, "level", 1)
    return current


def solution(mesh):
    in_specs = (
        P(("groups", "level"), None, None),
        P(("groups", "level")),
        P(("groups", "level")),
        P("groups"),
        P("level", None),
        P(),
        P(),
        P(),
        P(),
        P(),
        P(),
        P(),
        P(),
    )
    out_specs = P(("groups", "level"), None, None)
    return jax.shard_map(
        per_device, mesh=mesh, in_specs=in_specs, out_specs=out_specs, check_vma=False
    )
```

profile of v0, /device:TPU:25, one launch (start us, length us, event | category | flops | bytes accessed | tf_op | source)
XLA Modules:
  0.0 276.9 jit_solution(11633380892146557952)
XLA Ops:
  6.5 4.9 %fusion.33 = f32[77,1024]{1,0:T(8,128)} fusion(bf16[3088,1024]{1,0:T(8,128)(2,1)} %param.17, s32[3088]{0:T(1024)S(1)} %iota_add_fusion, s32[77]{0:T(128)} %param.16), kind=kOutput, calls=%fused_computation.84 | convolution fusion | flops 487203008 | bytes 6652276 | tf_op jit(solution)/shard_map/dot_general | solution.py:56
  11.5 89.9 %all-reduce.2.cloned.1.call-done = f32[77,1024]{1,0:T(8,128)} async-done(((f32[77,1024]{1,0:T(8,128)}), f32[77,1024]{1,0:T(8,128)}) %all-reduce.2.cloned.1.call-update) | async-done | bytes 315408 | tf_op jit(solution)/shard_map/psum | solution.py:57
  109.0 2.5 collective-permute-start
  113.5 2.1 convolution_convert_fusion.8
  116.7 2.0 reshape.375
  118.7 1.6 convert.37
  120.3 2.4 copy.96
  122.7 2.0 multiply_reduce_fusion.12
  124.7 15.7 %collective-permute-done = bf16[2,2,256,10,64]{2,4,3,1,0:T(8,128)(2,1)S(1)} collective-permute-done((bf16[2,2,256,10,64]{2,4,3,1,0:T(8,128)(2,1)}, bf16[2,2,256,10,64]{2,4,3,1,0:T(8,128)(2,1)S(1)}, u32[]{:S(2)}, u32[]{:S(2)}) %collective-permute-start) | collective-permute-done | bytes 1310752 | tf_op jit(solution)/shard_map/ppermute | solution.py:17
  140.5 9.4 %collective-permute-done.1 = bf16[2,2,256,10,64]{2,4,3,1,0:T(8,128)(2,1)S(1)} collective-permute-done((bf16[2,2,256,10,64]{2,4,3,1,0:T(8,128)(2,1)}, bf16[2,2,256,10,64]{2,4,3,1,0:T(8,128)(2,1)S(1)}, u32[]{:S(2)}, u32[]{:S(2)}) %collective-permute-start.1) | collective-permute-done | bytes 1310752 | tf_op jit(solution)/shard_map/ppermute | solution.py:20
  149.9 1.9 multiply_reduce_fusion.10
  156.4 7.5 %collective-permute-done.2 = bf16[2,256,640]{2,1,0:T(8,128)(2,1)S(1)} collective-permute-done((bf16[2,256,640]{2,1,0:T(8,128)(2,1)S(1)}, bf16[2,256,640]{2,1,0:T(8,128)(2,1)S(1)}, u32[]{:S(2)}, u32[]{:S(2)}) %collective-permute-start.2) | collective-permute-done | bytes 655392 | tf_op jit(solution)/shard_map/ppermute | solution.py:28
  169.3 2.5 collective-permute-start.3
  172.8 2.1 convolution_convert_fusion.5
  176.0 2.0 reshape.377
  178.1 1.6 convert.47
  179.6 2.4 copy.104
  182.0 2.0 multiply_reduce_fusion.7
  184.1 14.3 %collective-permute-done.3 = bf16[2,2,256,10,64]{2,4,3,1,0:T(8,128)(2,1)S(1)} collective-permute-done((bf16[2,2,256,10,64]{2,4,3,1,0:T(8,128)(2,1)}, bf16[2,2,256,10,64]{2,4,3,1,0:T(8,128)(2,1)S(1)}, u32[]{:S(2)}, u32[]{:S(2)}) %collective-permute-start.3) | collective-permute-done | bytes 1310752 | tf_op jit(solution)/shard_map/ppermute | solution.py:17
  198.3 4.2 %collective-permute-done.4 = bf16[2,2,256,10,64]{2,4,3,1,0:T(8,128)(2,1)S(1)} collective-permute-done((bf16[2,2,256,10,64]{2,4,3,1,0:T(8,128)(2,1)}, bf16[2,2,256,10,64]{2,4,3,1,0:T(8,128)(2,1)S(1)}, u32[]{:S(2)}, u32[]{:S(2)}) %collective-permute-start.4) | collective-permute-done | bytes 1310752 | tf_op jit(solution)/shard_map/ppermute | solution.py:20
  202.6 1.9 multiply_reduce_fusion.5
  209.2 7.5 %collective-permute-done.5 = bf16[2,256,640]{2,1,0:T(8,128)(2,1)S(1)} collective-permute-done((bf16[2,256,640]{2,1,0:T(8,128)(2,1)S(1)}, bf16[2,256,640]{2,1,0:T(8,128)(2,1)S(1)}, u32[]{:S(2)}, u32[]{:S(2)}) %collective-permute-start.5) | collective-permute-done | bytes 655392 | tf_op jit(solution)/shard_map/ppermute | solution.py:28
  222.1 2.5 collective-permute-start.6
  225.6 2.1 convolution_convert_fusion.2
  228.8 2.0 reshape.379
  230.8 1.6 convert.57
  232.4 2.4 copy.112
  234.8 2.0 multiply_reduce_fusion.2
  236.8 16.0 %collective-permute-done.6 = bf16[2,2,256,10,64]{2,4,3,1,0:T(8,128)(2,1)S(1)} collective-permute-done((bf16[2,2,256,10,64]{2,4,3,1,0:T(8,128)(2,1)}, bf16[2,2,256,10,64]{2,4,3,1,0:T(8,128)(2,1)S(1)}, u32[]{:S(2)}, u32[]{:S(2)}) %collective-permute-start.6) | collective-permute-done | bytes 1310752 | tf_op jit(solution)/shard_map/ppermute | solution.py:17
  252.9 2.4 collective-permute-done.7
  255.3 1.9 multiply_reduce_fusion
  261.7 7.5 %collective-permute-done.8 = bf16[2,256,640]{2,1,0:T(8,128)(2,1)S(1)} collective-permute-done((bf16[2,256,640]{2,1,0:T(8,128)(2,1)S(1)}, bf16[2,256,640]{2,1,0:T(8,128)(2,1)S(1)}, u32[]{:S(2)}, u32[]{:S(2)}) %collective-permute-start.8) | collective-permute-done | bytes 655392 | tf_op jit(solution)/shard_map/ppermute | solution.py:28
  (168 shorter events, 39.7 us)
Async XLA Ops:
  6.5 95.9 %copy-start = (bf16[1024,640]{1,0:T(8,128)(2,1)S(1)}, bf16[1024,640]{1,0:T(8,128)(2,1)}, u32[]{:S(2)}) copy-start(bf16[1024,640]{1,0:T(8,128)(2,1)} %param.18) | copy-start | bytes 3932164
  6.5 94.9 %all-reduce.2.cloned.1.call-start = ((), (), s32[]{:S(2)}) async-start(), calls=%async_computation | async-start | bytes 655360 | tf_op jit(solution)/shard_map/psum | solution.py:57
  11.5 91.2 %copy-start.31 = (f32[16,640]{1,0:T(8,128)S(1)}, f32[16,640]{1,0:T(8,128)}, u32[]{:S(2)}) copy-start(f32[16,640]{1,0:T(8,128)} %param.19) | copy-start | bytes 122884
  11.5 91.2 %copy-start.32 = (s32[2]{0:T(128)S(1)}, s32[2]{0:T(128)}, u32[]{:S(2)}) copy-start(s32[2]{0:T(128)} %param.14) | copy-start | bytes 28
  11.5 91.5 %copy-start.8 = (bf16[2,256,640]{2,1,0:T(8,128)(2,1)S(1)}, bf16[2,256,640]{2,1,0:T(8,128)(2,1)}, u32[]{:S(2)}) copy-start(bf16[2,256,640]{2,1,0:T(8,128)(2,1)} %param.13) | copy-start | bytes 1966084
  11.5 91.7 %copy-start.20 = (f32[640]{0:T(1024)S(1)}, f32[640]{0:T(1024)}, u32[]{:S(2)}) copy-start(f32[640]{0:T(1024)} %param.21) | copy-start | bytes 7684
  103.5 2.6 copy-start.17
  107.9 3.6 %copy-start.21 = (s32[2]{0:T(128)S(1)}, s32[2]{0:T(128)}, u32[]{:S(2)}) copy-start(s32[2]{0:T(128)} %param.15) | copy-start | bytes 28
  107.9 4.4 %copy-start.33 = (f32[16]{0:T(128)S(1)}, f32[16]{0:T(128)}, u32[]{:S(2)}) copy-start(f32[16]{0:T(128)} %param.20) | copy-start | bytes 196
  109.0 31.4 %collective-permute-start = (bf16[2,2,256,10,64]{2,4,3,1,0:T(8,128)(2,1)}, bf16[2,2,256,10,64]{2,4,3,1,0:T(8,128)(2,1)S(1)}, u32[]{:S(2)}, u32[]{:S(2)}) collective-permute-start(bf16[2,2,256,10,64]{2,4,3,1,0:T(8,128)(2,1)} %copy_dynamic-update-slice_fusion.4), channel_id=1, source_target_pairs={{0,1},{1,2},{2,3},{3,4},{4,5},{5,6},{6,7},{7,8},{8,9},{9,10},{10,1... | collective-permute-start | bytes 3932168 | tf_op jit(solution)/shard_map/ppermute | solution.py:17
  111.5 38.3 %collective-permute-start.1 = (bf16[2,2,256,10,64]{2,4,3,1,0:T(8,128)(2,1)}, bf16[2,2,256,10,64]{2,4,3,1,0:T(8,128)(2,1)S(1)}, u32[]{:S(2)}, u32[]{:S(2)}) collective-permute-start(bf16[2,2,256,10,64]{2,4,3,1,0:T(8,128)(2,1)} %copy_dynamic-update-slice_fusion.4), channel_id=1, source_target_pairs={{1,0},{2,1},{3,2},{4,3},{5,4},{6,5},{7,6},{8,7},{9,8},{10,9},{11,1... | collective-permute-start | bytes 3932168 | tf_op jit(solution)/shard_map/ppermute | solution.py:20
  122.7 27.2 %copy-start.5 = (f32[2,256,10,64]{1,0,3,2:T(2,128)S(1)}, f32[2,256,10,64]{1,0,3,2:T(2,128)}, u32[]{:S(2)}) copy-start(f32[2,256,10,64]{1,0,3,2:T(2,128)} %convert.37) | copy-start | bytes 3932164
  152.5 1.5 copy-start.3
  156.1 8.3 %copy-start.23 = (bf16[640,640]{1,0:T(8,128)(2,1)S(1)}, bf16[640,640]{1,0:T(8,128)(2,1)}, u32[]{:S(2)}) copy-start(bf16[640,640]{1,0:T(8,128)(2,1)} %param.23) | copy-start | bytes 2457604
  156.1 7.8 %collective-permute-start.2 = (bf16[2,256,640]{2,1,0:T(8,128)(2,1)S(1)}, bf16[2,256,640]{2,1,0:T(8,128)(2,1)S(1)}, u32[]{:S(2)}, u32[]{:S(2)}) collective-permute-start(bf16[2,256,640]{2,1,0:T(8,128)(2,1)S(1)} %fusion.6), channel_id=1, source_target_pairs={{15,0},{0,1},{1,2},{2,3},{3,4},{4,5},{5,6},{6,7},{7,8},{8,9},{9,10... | collective-permute-start | bytes 1966088 | tf_op jit(solution)/shard_map/ppermute | solution.py:28
  164.4 2.2 copy-start.19
  164.4 1.4 copy-start.26
  166.6 1.4 copy-start.15
  169.3 29.0 %collective-permute-start.3 = (bf16[2,2,256,10,64]{2,4,3,1,0:T(8,128)(2,1)}, bf16[2,2,256,10,64]{2,4,3,1,0:T(8,128)(2,1)S(1)}, u32[]{:S(2)}, u32[]{:S(2)}) collective-permute-start(bf16[2,2,256,10,64]{2,4,3,1,0:T(8,128)(2,1)} %copy_dynamic-update-slice_fusion.2), channel_id=1, source_target_pairs={{0,1},{1,2},{2,3},{3,4},{4,5},{5,6},{6,7},{7,8},{8,9},{9,10},{10,1... | collective-permute-start | bytes 3932168 | tf_op jit(solution)/shard_map/ppermute | solution.py:17
  171.8 30.8 %collective-permute-start.4 = (bf16[2,2,256,10,64]{2,4,3,1,0:T(8,128)(2,1)}, bf16[2,2,256,10,64]{2,4,3,1,0:T(8,128)(2,1)S(1)}, u32[]{:S(2)}, u32[]{:S(2)}) collective-permute-start(bf16[2,2,256,10,64]{2,4,3,1,0:T(8,128)(2,1)} %copy_dynamic-update-slice_fusion.2), channel_id=1, source_target_pairs={{1,0},{2,1},{3,2},{4,3},{5,4},{6,5},{7,6},{8,7},{9,8},{10,9},{11,1... | collective-permute-start | bytes 3932168 | tf_op jit(solution)/shard_map/ppermute | solution.py:20
  182.0 20.6 %copy-start.6 = (f32[2,256,10,64]{1,0,3,2:T(2,128)S(1)}, f32[2,256,10,64]{1,0,3,2:T(2,128)}, u32[]{:S(2)}) copy-start(f32[2,256,10,64]{1,0,3,2:T(2,128)} %convert.47) | copy-start | bytes 3932164
  205.2 1.5 copy-start.4
  208.9 8.3 %copy-start.24 = (bf16[640,640]{1,0:T(8,128)(2,1)S(1)}, bf16[640,640]{1,0:T(8,128)(2,1)}, u32[]{:S(2)}) copy-start(bf16[640,640]{1,0:T(8,128)(2,1)} %param.23) | copy-start | bytes 2457604
  208.9 7.8 %collective-permute-start.5 = (bf16[2,256,640]{2,1,0:T(8,128)(2,1)S(1)}, bf16[2,256,640]{2,1,0:T(8,128)(2,1)S(1)}, u32[]{:S(2)}, u32[]{:S(2)}) collective-permute-start(bf16[2,256,640]{2,1,0:T(8,128)(2,1)S(1)} %fusion.7), channel_id=1, source_target_pairs={{15,0},{0,1},{1,2},{2,3},{3,4},{4,5},{5,6},{6,7},{7,8},{8,9},{9,10... | collective-permute-start | bytes 1966088 | tf_op jit(solution)/shard_map/ppermute | solution.py:28
  217.2 2.2 copy-start.18
  219.4 1.4 copy-start.16
  222.1 30.8 %collective-permute-start.6 = (bf16[2,2,256,10,64]{2,4,3,1,0:T(8,128)(2,1)}, bf16[2,2,256,10,64]{2,4,3,1,0:T(8,128)(2,1)S(1)}, u32[]{:S(2)}, u32[]{:S(2)}) collective-permute-start(bf16[2,2,256,10,64]{2,4,3,1,0:T(8,128)(2,1)} %copy_dynamic-update-slice_fusion), channel_id=1, source_target_pairs={{0,1},{1,2},{2,3},{3,4},{4,5},{5,6},{6,7},{7,8},{8,9},{9,10},{10,1... | collective-permute-start | bytes 3932168 | tf_op jit(solution)/shard_map/ppermute | solution.py:17
  224.6 30.7 %collective-permute-start.7 = (bf16[2,2,256,10,64]{2,4,3,1,0:T(8,128)(2,1)}, bf16[2,2,256,10,64]{2,4,3,1,0:T(8,128)(2,1)S(1)}, u32[]{:S(2)}, u32[]{:S(2)}) collective-permute-start(bf16[2,2,256,10,64]{2,4,3,1,0:T(8,128)(2,1)} %copy_dynamic-update-slice_fusion), channel_id=1, source_target_pairs={{1,0},{2,1},{3,2},{4,3},{5,4},{6,5},{7,6},{8,7},{9,8},{10,9},{11,1... | collective-permute-start | bytes 3932168 | tf_op jit(solution)/shard_map/ppermute | solution.py:20
  234.8 20.6 %copy-start.7 = (f32[2,256,10,64]{1,0,3,2:T(2,128)S(1)}, f32[2,256,10,64]{1,0,3,2:T(2,128)}, u32[]{:S(2)}) copy-start(f32[2,256,10,64]{1,0,3,2:T(2,128)} %convert.57) | copy-start | bytes 3932164
  257.9 1.5 copy-start.2
  260.8 9.3 %copy-start.1 = (bf16[1024,640]{1,0:T(8,128)(2,1)S(1)}, bf16[1024,640]{1,0:T(8,128)(2,1)}, u32[]{:S(2)}) copy-start(bf16[1024,640]{1,0:T(8,128)(2,1)} %param.18) | copy-start | bytes 3932164
  261.6 7.6 %collective-permute-start.8 = (bf16[2,256,640]{2,1,0:T(8,128)(2,1)S(1)}, bf16[2,256,640]{2,1,0:T(8,128)(2,1)S(1)}, u32[]{:S(2)}, u32[]{:S(2)}) collective-permute-start(bf16[2,256,640]{2,1,0:T(8,128)(2,1)S(1)} %fusion.8), channel_id=1, source_target_pairs={{15,0},{0,1},{1,2},{2,3},{3,4},{4,5},{5,6},{6,7},{7,8},{8,9},{9,10... | collective-permute-start | bytes 1966088 | tf_op jit(solution)/shard_map/ppermute | solution.py:28
  (12 other events, 14.4 us)
Sparse Core Ops, SparseCore 0:
  11.6 89.7 all-reduce.1
where the time goes:
time: 282 us; the launch traced here: 277 us
  waiting for transfers between devices  175 us (62%)
  local copies, waits for them, and re-layouts  34.4 us (12%)
  other arithmetic  26.9 us (10%)
  matrix products  18.8 us (7%)
  between operations  14.1 us (5%)
  starting transfers between devices  8.04 us (3%)
    psum x1, waiting for transfers between devices, per_device(): pooled = jnp.mean(lax.psum(text_local, 'level'), axis=0)  89.9 us
    ppermute x3, waiting for transfers between devices, extended(): lax.ppermute(lax.slice_in_dim(block, block.shape[dim] - width, None, axis...  46.1 us
    ppermute x3, waiting for transfers between devices, shifted_2(): return lax.ppermute(block, axis, route)  22.6 us
    ppermute x3, waiting for transfers between devices, extended(): lax.ppermute(lax.slice_in_dim(block, 0, width, axis=dim), axis, backward)  16.1 us
    unnamed x18, other arithmetic  11.7 us
    dot_general x9, matrix products, project(): jnp.dot(flat, weight, preferred_element_type=jnp.float32)  10.8 us
    unnamed x72, local copies, waits for them, and re-layouts  8.87 us
    ppermute x3, starting transfers between devices, extended(): lax.ppermute(lax.slice_in_dim(block, block.shape[dim] - width, None, axis...  7.46 us
  transfers between devices with their start and end apart: 10, of which 10 were waited for; matrix products, arithmetic and copies ran while one was open for 14% of the time, Pallas kernels for 0%

commit v1 on v0

v1 whole, which is shorter than its diff:
```python
import functools

import jax
import jax.numpy as jnp
from jax import lax
from jax.experimental import pallas as pl
from jax.experimental.pallas import tpu as pltpu
from jax.sharding import PartitionSpec as P

DH = 64
BAND = 2
STEPS = 3
SPAN = 2 * BAND + 1
MESH = pl.DeviceIdType.MESH


def queue_kernel(
    n,
    group,
    tokens_text,
    x_hbm,
    meta_ref,
    ids_ref,
    table_hbm,
    proj_hbm,
    embed_ref,
    srate_ref,
    gain_ref,
    wq_hbm,
    wk_hbm,
    wv_hbm,
    wo_hbm,
    out_hbm,
    recv,
    xa,
    xb,
    xo,
    normed,
    q_s,
    k_s,
    v_s,
    att_s,
    table,
    proj,
    wq,
    wk,
    wv,
    wo,
    pool,
    metas,
    cond,
    rate,
    mask,
    fold,
    unfold,
    x_send,
    x_recv,
    p_send,
    p_recv,
    m_send,
    m_recv,
    o_send,
    o_recv,
    local,
):
    me = lax.axis_index("level")
    fdev = x_hbm.shape[0]
    frames, pos, width = recv.shape
    barrier = pltpu.get_barrier_semaphore()
    for hop in range(1, n):
        pl.semaphore_signal(
            barrier, inc=1, device_id={"level": lax.rem(me + hop, n)}, device_id_type=MESH
        )
    stage = [
        pltpu.make_async_copy(src, dst, local.at[slot])
        for slot, (src, dst) in enumerate(
            (
                (table_hbm, table),
                (proj_hbm, proj),
                (wq_hbm, wq),
                (wk_hbm, wk),
                (wv_hbm, wv),
                (wo_hbm, wo),
                (x_hbm.at[:, me], recv.at[pl.ds(me * fdev, fdev)]),
                (meta_ref, metas.at[me]),
            )
        )
    ]
    for copy in stage:
        copy.start()
    pl.semaphore_wait(barrier, n - 1)

    def x_copy(peer, owner):
        return pltpu.make_async_remote_copy(
            src_ref=x_hbm.at[:, peer],
            dst_ref=recv.at[pl.ds(owner * fdev, fdev)],
            send_sem=x_send.at[peer],
            recv_sem=x_recv.at[owner],
            device_id={"level": peer},
            device_id_type=MESH,
        )

    def p_copy(peer, owner):
        return pltpu.make_async_remote_copy(
            src_ref=pool.at[owner],
            dst_ref=pool.at[owner],
            send_sem=p_send.at[peer],
            recv_sem=p_recv.at[owner],
            device_id={"level": peer},
            device_id_type=MESH,
        )

    def m_copy(peer, owner):
        return pltpu.make_async_remote_copy(
            src_ref=meta_ref,
            dst_ref=metas.at[owner],
            send_sem=m_send.at[peer],
            recv_sem=m_recv.at[owner],
            device_id={"level": peer},
            device_id_type=MESH,
        )

    peers = [lax.rem(me + hop, n) for hop in range(1, n)]
    for peer in peers:
        m_copy(peer, me).start()
    half = (n - 1) // 2
    for peer in peers[:half]:
        x_copy(peer, me).start()

    vocab = table.shape[0]
    own = ids_ref[...] - me * vocab
    hits = lax.broadcasted_iota(jnp.int32, (tokens_text, vocab), 1) == own
    counts = jnp.sum(hits.astype(jnp.float32), axis=0, keepdims=True)
    counts = jnp.broadcast_to(counts, (16, vocab)).astype(jnp.bfloat16)
    stage[0].wait()
    partial = jnp.dot(counts, table[...], preferred_element_type=jnp.float32)
    pool[me] = partial[0:1]
    for peer in peers:
        p_copy(peer, me).start()
    for peer in peers[half:]:
        x_copy(peer, me).start()

    heads = width // DH
    row = lax.broadcasted_iota(jnp.int32, (width, 128), 0)
    col = lax.broadcasted_iota(jnp.int32, (width, 128), 1) * DH
    fold[...] = ((row >= col) & (row < col + DH)).astype(jnp.float32).astype(jnp.bfloat16)
    row = lax.broadcasted_iota(jnp.int32, (128, width), 0) * DH
    col = lax.broadcasted_iota(jnp.int32, (128, width), 1)
    unfold[...] = ((col >= row) & (col < row + DH)).astype(jnp.float32).astype(jnp.bfloat16)
    edge = jnp.zeros((BAND, pos, width), jnp.bfloat16)
    for buffer in (k_s, v_s):
        buffer[0:BAND] = edge
        buffer[frames + BAND : frames + 2 * BAND] = edge

    stage[7].wait()
    for peer in peers:
        m_copy(peer, peer).wait_recv()
    facts = metas[...].reshape(n, 128)
    slot_index = lax.broadcasted_iota(jnp.int32, (n, 128), 0)
    bases = []
    for f in range(fdev):
        level = facts[:, f : f + 1]
        base = jnp.zeros((n, width), jnp.float32)
        speed = jnp.zeros((n, width), jnp.float32)
        for number in range(embed_ref.shape[0]):
            chosen = level == float(number)
            base = base + jnp.where(chosen, embed_ref[number : number + 1, :], 0.0)
            speed = speed + jnp.where(chosen, srate_ref[0:1, number : number + 1], 0.0)
        bases.append(base)
        reach = jnp.broadcast_to(facts[:, fdev + f : fdev + f + 1], (n, 128))
        spot = slot_index * fdev + f
        for s in range(n):
            rate[s * fdev + f] = speed[s : s + 1]
        for slot in range(SPAN):
            offset = slot - BAND
            valid = (
                (reach >= float(-offset)) & (spot + offset >= 0) & (spot + offset < frames)
            ).astype(jnp.float32)
            for s in range(n):
                mask[slot, s * fdev + f] = valid[s : s + 1]

    stage[1].wait()
    for peer in peers:
        p_copy(peer, peer).wait_recv()
    pooled = jnp.sum(pool[...], axis=0) / float(tokens_text)
    pooled = jnp.broadcast_to(pooled, (16, pooled.shape[1])).astype(jnp.bfloat16)
    text = jnp.dot(pooled, proj[...], preferred_element_type=jnp.float32)[0:1]
    for f in range(fdev):
        full = bases[f] + text
        for s in range(n):
            cond[s * fdev + f] = full[s : s + 1]

    for slot in (2, 3, 4, 5, 6):
        stage[slot].wait()
    for peer in peers:
        x_copy(peer, peer).wait_recv()

    rows = group * pos
    gain = gain_ref[...].reshape(1, 1, width)

    def project(source):
        def body(index, carry):
            at = pl.ds(index * group, group)
            hin = source[at].astype(jnp.float32) + cond[at]
            power = jnp.mean(hin * hin, axis=-1, keepdims=True)
            flat = (hin * lax.rsqrt(power + 1e-06) * gain).astype(jnp.bfloat16).reshape(rows, width)
            there = pl.ds(index * group + BAND, group)
            for weight, target, spot in ((wq, q_s, at), (wk, k_s, there), (wv, v_s, there)):
                target[spot] = (
                    jnp.dot(flat, weight[...], preferred_element_type=jnp.float32)
                    .astype(jnp.bfloat16)
                    .reshape(group, pos, width)
                )
            return carry

        lax.fori_loop(0, frames // group, body, 0)

    def attend(source, target, lead):
        scale = 1.0 / DH**0.5

        def body(index, carry):
            first = index * group
            at = pl.ds(first, group)
            query = q_s[at].reshape(rows, width)
            scores = []
            masks = []
            for slot in range(SPAN):
                keys = k_s[pl.ds(first + slot, group)].reshape(rows, width)
                raw = jnp.dot(query * keys, fold[...], preferred_element_type=jnp.float32) * scale
                valid = mask[slot, at]
                raw = jnp.where(valid > 0.0, raw.reshape(group, pos, 128), -1e30)
                scores.append(raw)
                masks.append(valid)
            top = functools.reduce(jnp.maximum, scores)
            expo = [jnp.exp(score - top) * valid for score, valid in zip(scores, masks)]
            inverse = 1.0 / functools.reduce(jnp.add, expo)
            total = None
            for slot in range(SPAN):
                weight = (expo[slot] * inverse).astype(jnp.bfloat16).reshape(rows, 128)
                spread = jnp.dot(weight, unfold[...], preferred_element_type=jnp.float32)
                values = v_s[pl.ds(first + slot, group)].reshape(rows, width)
                term = spread * values.astype(jnp.float32)
                total = term if total is None else total + term
            noise = jnp.dot(
                total.astype(jnp.bfloat16), wo[...], preferred_element_type=jnp.float32
            ).reshape(group, pos, width)
            fresh = source[at].astype(jnp.float32) - rate[at] * noise
            target[pl.ds(first + lead, group)] = fresh.astype(jnp.bfloat16)
            return carry

        lax.fori_loop(0, frames // group, body, 0)

    buffers = (recv, xa, xb, xo)
    for step in range(STEPS):
        source, target = buffers[step], buffers[step + 1]
        last = step == STEPS - 1
        project(source)
        attend(source, target, 0 if last else fdev)
        if not last:
            target[0:fdev] = target[frames : frames + fdev]

    def o_copy(section, owner, peer):
        return pltpu.make_async_remote_copy(
            src_ref=xo.at[pl.ds(section * fdev, fdev)],
            dst_ref=out_hbm.at[:, owner],
            send_sem=o_send.at[peer],
            recv_sem=o_recv.at[owner],
            device_id={"level": peer},
            device_id_type=MESH,
        )

    for peer in peers:
        o_copy(lax.rem(peer + n - 1, n), me, peer).start()
    keep = pltpu.make_async_copy(
        xo.at[pl.ds(lax.rem(me + n - 1, n) * fdev, fdev)], out_hbm.at[:, me], local.at[8]
    )
    keep.start()
    keep.wait()
    for peer in peers:
        x_copy(peer, me).wait_send()
        m_copy(peer, me).wait_send()
        p_copy(peer, me).wait_send()
    for peer in peers:
        o_copy(lax.rem(peer + n - 1, n), me, peer).wait_send()
        o_copy(lax.rem(me + n - 1, n), peer, me).wait_recv()


def fused(
    latents,
    levels,
    back_reach,
    text_ids,
    text_table,
    text_proj,
    level_embed,
    step_rate,
    norm_gain,
    w_query,
    w_key,
    w_value,
    w_out,
):
    n = lax.axis_size("level")
    fdev, tokens, width = latents.shape
    pos = tokens // n
    frames = fdev * n
    group = frames // 2
    bf16, f32 = jnp.bfloat16, jnp.float32
    meta = jnp.concatenate([levels, back_reach]).astype(f32)
    meta = jnp.pad(meta, (0, 128 - 2 * fdev))[None, :]
    srate = jnp.pad(step_rate, (0, 128 - step_rate.shape[0]))[None, :]
    anywhere = pl.BlockSpec(memory_space=pl.ANY)
    vmem = pl.BlockSpec(memory_space=pltpu.VMEM)
    dma = pltpu.SemaphoreType.DMA
    block = (frames, pos, width)
    out = pl.pallas_call(
        functools.partial(queue_kernel, n, group, text_ids.shape[0]),
        out_shape=jax.ShapeDtypeStruct((fdev, n, pos, width), bf16),
        in_specs=[
            anywhere,
            vmem,
            vmem,
            anywhere,
            anywhere,
            vmem,
            vmem,
            vmem,
            anywhere,
            anywhere,
            anywhere,
            anywhere,
        ],
        out_specs=anywhere,
        scratch_shapes=[
            pltpu.VMEM(block, bf16),
            pltpu.VMEM((frames + fdev, pos, width), bf16),
            pltpu.VMEM((frames + fdev, pos, width), bf16),
            pltpu.VMEM(block, bf16),
            pltpu.VMEM((8, 128), bf16),
            pltpu.VMEM(block, bf16),
            pltpu.VMEM((frames + 2 * BAND, pos, width), bf16),
            pltpu.VMEM((frames + 2 * BAND, pos, width), bf16),
            pltpu.VMEM((8, 128), bf16),
            pltpu.VMEM(text_table.shape, bf16),
            pltpu.VMEM(text_proj.shape, bf16),
            pltpu.VMEM(w_query.shape, bf16),
            pltpu.VMEM(w_key.shape, bf16),
            pltpu.VMEM(w_value.shape, bf16),
            pltpu.VMEM(w_out.shape, bf16),
            pltpu.VMEM((n, 1, text_table.shape[1]), f32),
            pltpu.VMEM((n, 1, 128), f32),
            pltpu.VMEM((frames, 1, width), f32),
            pltpu.VMEM((frames, 1, width), f32),
            pltpu.VMEM((SPAN, frames, 1, 128), f32),
            pltpu.VMEM((width, 128), bf16),
            pltpu.VMEM((128, width), bf16),
            dma((n,)),
            dma((n,)),
            dma((n,)),
            dma((n,)),
            dma((n,)),
            dma((n,)),
            dma((n,)),
            dma((n,)),
            dma((9,)),
        ],
        compiler_params=pltpu.CompilerParams(
            collective_id=0, has_side_effects=True, vmem_limit_bytes=60 << 20
        ),
        name="queue",
    )(
        latents.reshape(fdev, n, pos, width),
        meta,
        text_ids[:, None],
        text_table,
        text_proj,
        level_embed,
        srate,
        norm_gain[None, :],
        w_query,
        w_key,
        w_value,
        w_out,
    )
    return out.reshape(fdev, tokens, width)


def general(
    latents,
    levels,
    back_reach,
    text_ids,
    text_table,
    text_proj,
    level_embed,
    step_rate,
    norm_gain,
    w_query,
    w_key,
    w_value,
    w_out,
):
    n = lax.axis_size("level")
    index = lax.axis_index("level")
    fdev, tokens, width = latents.shape
    heads = width // DH
    frames = fdev * n
    vocab = text_table.shape[0]
    spots = index * vocab + jnp.arange(vocab, dtype=jnp.int32)
    counts = jnp.sum((text_ids[:, None] == spots[None, :]).astype(jnp.float32), axis=0)
    partial = jnp.dot(
        counts.astype(jnp.bfloat16)[None, :], text_table, preferred_element_type=jnp.float32
    )
    pooled = lax.psum(partial, "level") / text_ids.shape[0]
    text_vec = jnp.dot(pooled.astype(jnp.bfloat16), text_proj, preferred_element_type=jnp.float32)
    levels = lax.all_gather(levels, "level", tiled=True)
    reach = lax.all_gather(back_reach, "level", tiled=True)
    cond = level_embed[levels] + text_vec
    rate = step_rate[levels]
    current = lax.all_to_all(latents, "level", split_axis=1, concat_axis=0, tiled=True)
    pos = tokens // n
    spot = jnp.arange(frames, dtype=jnp.int32)
    for step in range(STEPS):
        hin = current.astype(jnp.float32) + cond[:, None, :]
        power = jnp.mean(hin * hin, axis=-1, keepdims=True)
        normed = (hin * lax.rsqrt(power + 1e-06) * norm_gain).astype(jnp.bfloat16)
        flat = normed.reshape(-1, width)

        def project(weight):
            out = jnp.dot(flat, weight, preferred_element_type=jnp.float32)
            return out.astype(jnp.bfloat16).reshape(frames, pos, heads, DH).astype(jnp.float32)

        edge = ((BAND, BAND), (0, 0), (0, 0), (0, 0))
        query = project(w_query)
        keys = jnp.pad(project(w_key), edge)
        values = jnp.pad(project(w_value), edge)
        scores = []
        masks = []
        for offset in range(-BAND, BAND + 1):
            raw = jnp.sum(query * keys[BAND + offset : BAND + offset + frames], -1) / DH**0.5
            valid = (offset >= -reach) & (spot + offset >= 0) & (spot + offset < frames)
            scores.append(jnp.where(valid[:, None, None], raw, -1e30))
            masks.append(valid.astype(jnp.float32)[:, None, None])
        scores = jnp.stack(scores)
        expo = jnp.exp(scores - jnp.max(scores, axis=0)[None]) * jnp.stack(masks)
        weights = (expo / jnp.sum(expo, axis=0)[None]).astype(jnp.bfloat16).astype(jnp.float32)
        attended = jnp.zeros((frames, pos, heads, DH), jnp.float32)
        for slot in range(SPAN):
            attended = attended + weights[slot][..., None] * values[slot : slot + frames]
        noise = jnp.dot(
            attended.astype(jnp.bfloat16).reshape(-1, width),
            w_out,
            preferred_element_type=jnp.float32,
        ).reshape(frames, pos, width)
        updated = current.astype(jnp.float32) - rate[:, None, None] * noise
        current = jnp.roll(updated.astype(jnp.bfloat16), fdev, axis=0)
    return lax.all_to_all(current, "level", split_axis=0, concat_axis=1, tiled=True)


def per_device(latents, *rest):
    n = lax.axis_size("level")
    tokens = latents.shape[1]
    if tokens % (16 * n) == 0:
        return fused(latents, *rest)
    return general(latents, *rest)


def solution(mesh):
    in_specs = (
        P(("groups", "level"), None, None),
        P(("groups", "level")),
        P(("groups", "level")),
        P("groups"),
        P("level", None),
        P(),
        P(),
        P(),
        P(),
        P(),
        P(),
        P(),
        P(),
    )
    out_specs = P(("groups", "level"), None, None)
    return jax.shard_map(
        per_device, mesh=mesh, in_specs=in_specs, out_specs=out_specs, check_vma=False
    )
```

time: 282 us -> 61.8 us (0.22); the launches traced: 277 us -> 60.7 us
  waiting for transfers between devices: 175 us -> 0 us
  Pallas kernels: 0 us -> 54.1 us
  local copies, waits for them, and re-layouts: 34.4 us -> 5.81 us
  other arithmetic: 26.9 us -> 0.75 us
  matrix products: 18.8 us -> 0 us
  between operations: 14.1 us -> 0.01 us
  starting transfers between devices: 8.04 us -> 0 us
    psum x1 -> x0, waiting for transfers between devices: 89.9 us -> none  [per_device(): pooled = jnp.mean(lax.psum(text_local, 'level'), axis=0)]
    ppermute x9 -> x0, waiting for transfers between devices: 84.7 us -> none  [the longest x3 46.1 us: extended(): lax.ppermute(lax.slice_in_dim(block, block.shape[dim] - width, None, axis...]
    pallas_call x0 -> x1, Pallas kernels: none -> 54.1 us  [fused(): pl.pallas_call(functools.partial(queue_kernel, n, group, text_ids.shape[0...]
    dot_general x16 -> x0, matrix products: 18.8 us -> none  [the longest x9 10.8 us: project(): jnp.dot(flat, weight, preferred_element_type=jnp.float32)]
    convert_element_type x13 -> x0, local copies, waits for them, and re-layouts: 12 us -> none  [the longest x3 7.16 us: per_device(): shifted.astype(jnp.float32)]
    unnamed x18 -> x0, other arithmetic: 11.7 us -> none
    ppermute x9 -> x0, starting transfers between devices: 8.04 us -> none  [the longest x3 7.46 us: extended(): lax.ppermute(lax.slice_in_dim(block, block.shape[dim] - width, None, axis...]
    unnamed x72 -> x1, local copies, waits for them, and re-layouts: 8.87 us -> 1.98 us
  transfers between devices with their start and end apart: 10 -> 0, of which waited for: 10 -> 0; matrix products, arithmetic and copies ran while one was open for 14% -> 0% of each run, Pallas kernels for 0% -> 0%
where the time goes in v1:
time: 61.8 us; the launch traced here: 60.7 us
  Pallas kernels  54.1 us (88%)
  local copies, waits for them, and re-layouts  5.81 us (9%)
  other arithmetic  0.75 us (1%)
    pallas_call x1, Pallas kernels, fused(): pl.pallas_call(functools.partial(queue_kernel, n, group, text_ids.shape[0...  54.1 us
    unnamed x1, local copies, waits for them, and re-layouts  1.98 us
    broadcast_in_dim x1, local copies, waits for them, and re-layouts, fused(): text_ids[:, None]  1.37 us
    broadcast_in_dim x1, local copies, waits for them, and re-layouts, fused(): norm_gain[None, :]  1.27 us

profile of v1, /device:TPU:25, one launch (start us, length us, event | category | flops | bytes accessed | tf_op | source)
XLA Modules:
  0.0 60.7 jit_solution(3731108559166304277)
XLA Ops:
  0.0 0.7 %add_convert_fusion = f32[4]{0:T(128)S(1)} fusion(s32[2]{0:T(128)} %param.15, s32[2]{0:T(128)} %param.14), kind=kLoop, calls=%fused_computation | loop fusion | flops 8 | bytes 32 | tf_op jit(solution)/shard_map/convert_element_type | solution.py:309
  0.7 1.2 %pad_bitcast_fusion = (f32[1,128]{1,0:T(1,128)}, f32[1,128]{1,0:T(1,128)}) fusion(f32[16]{0:T(128)} %param.20, f32[4]{0:T(128)S(1)} %add_convert_fusion), kind=kLoop, calls=%fused_computation.1 | loop fusion | bytes 1104 | tf_op jit(solution)/shard_map/broadcast_in_dim | solution.py:311
  1.9 1.3 %broadcast_in_dim.15.gain_ref = f32[1,640]{1,0:T(1,128)} reshape(f32[640]{0:T(1024)} %param.21) | data formatting | bytes 5120 | tf_op jit(solution)/shard_map/broadcast_in_dim | solution.py:379
  3.2 1.4 %copy.14.ids_ref = s32[77,1]{1,0:T(8,128)} copy(s32[77,1]{0,1:T(1,128)} %bitcast.9) | data formatting | bytes 616 | tf_op jit(solution)/shard_map/broadcast_in_dim | solution.py:374
  4.6 54.1 %queue.1 = bf16[2,16,16,640]{3,2,1,0:T(8,128)(2,1)} custom-call(bf16[2,16,16,640]{3,2,1,0:T(8,128)(2,1)} %bitcast.8, f32[1,128]{1,0:T(1,128)} %get-tuple-element.6.meta_ref, s32[77,1]{1,0:T(8,128)} %copy.14.ids_ref, bf16[3088,1024]{1,0:T(8,128)(2,1)} %table_hbm.1, bf16[1024,640]{1,0:T(8,128)(2,1)} %proj_hbm.1, f32[16,640]{1,0:T(8,128)} %embed_ref.1, ...), custom_call_target="tpu_custom_call" | custom-call | tf_op jit(solution)/shard_map/queue/pallas_call | solution.py:316
  58.7 2.0 %copy.16 = bf16[2,256,640]{2,1,0:T(8,128)(2,1)} copy(bf16[2,256,640]{2,1,0:T(8,128)(2,1)} %bitcast.7) | data formatting | bytes 1310720

commit v2 on v1

v2 whole, which is shorter than its diff:
```python
import functools

import jax
import jax.numpy as jnp
from jax import lax
from jax.experimental import pallas as pl
from jax.experimental.pallas import tpu as pltpu
from jax.sharding import PartitionSpec as P

DH = 64
BAND = 2
STEPS = 3
SPAN = 2 * BAND + 1
MESH = pl.DeviceIdType.MESH


def queue_kernel(
    n,
    blocks,
    x_hbm,
    level_hbm,
    reach_hbm,
    ids_hbm,
    table_hbm,
    proj_hbm,
    embed_hbm,
    srate_hbm,
    gain_hbm,
    wq_hbm,
    wk_hbm,
    wv_hbm,
    wo_hbm,
    out_hbm,
    recv,
    xa,
    xb,
    xo,
    q_s,
    k_even,
    k_odd,
    v_even,
    v_odd,
    table,
    proj,
    embed,
    gain_s,
    wq,
    wk,
    wv,
    wo,
    level_s,
    reach_s,
    ids_s,
    srate_s,
    pool,
    metas,
    cond,
    rate,
    mask,
    fold,
    unfold,
    x_send,
    x_recv,
    p_send,
    p_recv,
    m_send,
    m_recv,
    o_send,
    o_recv,
    local,
):
    me = lax.axis_index("level")
    fdev = x_hbm.shape[0]
    halves, frames, pos, width = recv.shape
    rows = frames * pos
    pad = BAND * pos
    barrier = pltpu.get_barrier_semaphore()
    for hop in range(1, n):
        pl.semaphore_signal(
            barrier, inc=1, device_id={"level": lax.rem(me + hop, n)}, device_id_type=MESH
        )
    mine = pl.ds(me * fdev, fdev)
    pairs = [
        (level_hbm, level_s),
        (reach_hbm, reach_s),
        (ids_hbm, ids_s),
        (srate_hbm, srate_s),
        (table_hbm, table),
        (embed_hbm, embed),
        (gain_hbm, gain_s),
        (proj_hbm, proj),
        (wq_hbm, wq),
        (wk_hbm, wk),
        (wv_hbm, wv),
        (wo_hbm, wo),
    ] + [(x_hbm.at[:, me, h], recv.at[h, mine]) for h in range(halves)]
    stage = [
        pltpu.make_async_copy(src, dst, local.at[slot]) for slot, (src, dst) in enumerate(pairs)
    ]
    for copy in stage:
        copy.start()

    def x_copy(h, peer, owner):
        return pltpu.make_async_remote_copy(
            src_ref=x_hbm.at[:, peer, h],
            dst_ref=recv.at[h, pl.ds(owner * fdev, fdev)],
            send_sem=x_send.at[h, peer],
            recv_sem=x_recv.at[h, owner],
            device_id={"level": peer},
            device_id_type=MESH,
        )

    def p_copy(peer, owner):
        return pltpu.make_async_remote_copy(
            src_ref=pool.at[owner],
            dst_ref=pool.at[owner],
            send_sem=p_send.at[peer],
            recv_sem=p_recv.at[owner],
            device_id={"level": peer},
            device_id_type=MESH,
        )

    def m_copy(peer, owner):
        return pltpu.make_async_remote_copy(
            src_ref=metas.at[owner],
            dst_ref=metas.at[owner],
            send_sem=m_send.at[peer],
            recv_sem=m_recv.at[owner],
            device_id={"level": peer},
            device_id_type=MESH,
        )

    def o_copy(h, section, owner, peer):
        return pltpu.make_async_remote_copy(
            src_ref=xo.at[h, pl.ds(section * fdev, fdev)],
            dst_ref=out_hbm.at[:, owner, h],
            send_sem=o_send.at[h, peer],
            recv_sem=o_recv.at[h, owner],
            device_id={"level": peer},
            device_id_type=MESH,
        )

    peers = [lax.rem(me + hop, n) for hop in range(1, n)]
    pl.semaphore_wait(barrier, n - 1)
    for peer in peers:
        x_copy(0, peer, me).start()

    stage[0].wait()
    stage[1].wait()
    lane = lax.broadcasted_iota(jnp.int32, (1, 128), 1)
    fact = jnp.zeros((1, 128), jnp.int32)
    for f in range(fdev):
        fact = jnp.where(lane == f, level_s[f], fact)
        fact = jnp.where(lane == fdev + f, reach_s[f], fact)
    metas[me] = fact
    for peer in peers:
        m_copy(peer, me).start()

    vocab = table.shape[0]
    stage[2].wait()
    first_id = me * vocab
    spots = lax.broadcasted_iota(jnp.int32, (1, vocab), 1) + first_id
    counts = jnp.zeros((1, vocab), jnp.float32)
    text_tokens = ids_s.shape[0]
    for token in range(text_tokens):
        counts = counts + jnp.where(spots == ids_s[token], 1.0, 0.0)
    counts = jnp.broadcast_to(counts, (16, vocab)).astype(jnp.bfloat16)
    stage[4].wait()
    partial = jnp.dot(counts, table[...], preferred_element_type=jnp.float32)
    pool[me] = partial[0:1]
    for peer in peers:
        p_copy(peer, me).start()
    for h in range(1, halves):
        for peer in peers:
            x_copy(h, peer, me).start()

    row = lax.broadcasted_iota(jnp.int32, (width, 128), 0)
    col = lax.broadcasted_iota(jnp.int32, (width, 128), 1) * DH
    fold[...] = ((row >= col) & (row < col + DH)).astype(jnp.float32).astype(jnp.bfloat16)
    row = lax.broadcasted_iota(jnp.int32, (128, width), 0) * DH
    col = lax.broadcasted_iota(jnp.int32, (128, width), 1)
    unfold[...] = ((col >= row) & (col < row + DH)).astype(jnp.float32).astype(jnp.bfloat16)
    edge = jnp.zeros((pad, width), jnp.bfloat16)
    for buffer in (k_even, v_even):
        buffer[0:pad] = edge
        buffer[rows + pad : rows + 2 * pad] = edge

    for slot in (3, 5, 6, 7):
        stage[slot].wait()
    for peer in peers:
        m_copy(peer, peer).wait_recv()
    facts = metas[...].reshape(n, 128)
    slot_index = lax.broadcasted_iota(jnp.int32, (n, 128), 0)
    bases = []
    for f in range(fdev):
        level = facts[:, f : f + 1]
        base = jnp.zeros((n, width), jnp.float32)
        speed = jnp.zeros((n, width), jnp.float32)
        for number in range(embed.shape[0]):
            chosen = level == number
            base = base + jnp.where(chosen, embed[number : number + 1, :], 0.0)
            speed = speed + jnp.where(chosen, srate_s[number], 0.0)
        bases.append(base)
        reach = jnp.broadcast_to(facts[:, fdev + f : fdev + f + 1], (n, 128))
        spot = slot_index * fdev + f
        for s in range(n):
            rate[s * fdev + f] = speed[s : s + 1]
        for slot in range(SPAN):
            offset = slot - BAND
            valid = ((reach >= -offset) & (spot + offset >= 0) & (spot + offset < frames)).astype(
                jnp.float32
            )
            for s in range(n):
                mask[slot, s * fdev + f] = valid[s : s + 1]

    for peer in peers:
        p_copy(peer, peer).wait_recv()
    pooled = jnp.sum(pool[...], axis=0) / float(text_tokens)
    pooled = jnp.broadcast_to(pooled, (16, pooled.shape[1])).astype(jnp.bfloat16)
    text = jnp.dot(pooled, proj[...], preferred_element_type=jnp.float32)[0:1]
    for f in range(fdev):
        full = bases[f] + text
        for s in range(n):
            cond[s * fdev + f] = full[s : s + 1]

    for slot in (8, 9, 10, 11):
        stage[slot].wait()

    gain = gain_s[...].reshape(1, 1, width)
    scale = 1.0 / DH**0.5
    group = frames // blocks
    size = group * pos

    def project(current):
        hin = current + cond[...]
        power = jnp.mean(hin * hin, axis=-1, keepdims=True)
        flat = (hin * lax.rsqrt(power + 1e-06) * gain).reshape(rows, width).astype(jnp.bfloat16)
        q_s[...] = jnp.dot(flat, wq[...], preferred_element_type=jnp.float32).astype(jnp.bfloat16)
        fill = jnp.zeros((pos, width), jnp.float32)
        for weight, even, odd in ((wk, k_even, k_odd), (wv, v_even, v_odd)):
            made = jnp.dot(flat, weight[...], preferred_element_type=jnp.float32)
            even[pad : pad + rows] = made.astype(jnp.bfloat16)
            odd[0 : rows + 2 * pos] = jnp.concatenate([fill, made, fill], axis=0).astype(
                jnp.bfloat16
            )

    def attend(first, current):
        at = pl.ds(first, group)
        start = first * pos

        def shifted(even, odd, slot):
            source = even if slot % 2 == 0 else odd
            return source[pl.ds(pl.multiple_of(start + (slot - slot % 2) * pos, 16), size)]

        query = q_s[pl.ds(pl.multiple_of(start, 16), size)]
        scores = []
        masks = []
        for slot in range(SPAN):
            keys = shifted(k_even, k_odd, slot)
            raw = jnp.dot(query * keys, fold[...], preferred_element_type=jnp.float32) * scale
            valid = mask[slot, at]
            scores.append(jnp.where(valid > 0.0, raw.reshape(group, pos, 128), -1e30))
            masks.append(valid)
        top = functools.reduce(jnp.maximum, scores)
        expo = [jnp.exp(score - top) * valid for score, valid in zip(scores, masks)]
        inverse = 1.0 / functools.reduce(jnp.add, expo)
        total = None
        for slot in range(SPAN):
            weight = (expo[slot] * inverse).reshape(size, 128).astype(jnp.bfloat16)
            spread = jnp.dot(weight, unfold[...], preferred_element_type=jnp.float32)
            term = spread * shifted(v_even, v_odd, slot).astype(jnp.float32)
            total = term if total is None else total + term
        noise = jnp.dot(total.astype(jnp.bfloat16), wo[...], preferred_element_type=jnp.float32)
        return current - rate[at] * noise.reshape(group, pos, width)

    def half(h, carry):
        stage_x = pltpu.make_async_copy(x_hbm.at[:, me, h], recv.at[h, mine], local.at[12 + h])
        stage_x.wait()
        for peer in peers:
            x_copy(h, peer, peer).wait_recv()
        turn = fdev * pos
        for step in range(STEPS):
            last = step == STEPS - 1
            held = xa if step % 2 == 1 else xb
            fresh = xb if step % 2 == 1 else xa

            def load(first, count, step=step, held=held):
                if step == 0:
                    return recv[h, pl.ds(first, count)].astype(jnp.float32)
                start = pl.multiple_of(first * pos, 16)
                return (
                    held[pl.ds(start, count * pos)].astype(jnp.float32).reshape(count, pos, width)
                )

            project(load(0, frames))

            def body(index, carry, load=load, fresh=fresh, last=last):
                first = index * group
                made = attend(first, load(first, group))
                if last:
                    xo[h, pl.ds(first, group)] = made.astype(jnp.bfloat16)
                else:
                    spot = pl.multiple_of(first * pos + turn, 16)
                    fresh[pl.ds(spot, size)] = made.reshape(size, width).astype(jnp.bfloat16)
                return carry

            lax.fori_loop(0, blocks, body, 0)
            if not last:
                fresh[0:turn] = fresh[rows : rows + turn]
        for peer in peers:
            o_copy(h, lax.rem(peer + n - 1, n), me, peer).start()
        pltpu.make_async_copy(
            xo.at[h, pl.ds(lax.rem(me + n - 1, n) * fdev, fdev)],
            out_hbm.at[:, me, h],
            local.at[12 + halves + h],
        ).start()
        return carry

    lax.fori_loop(0, halves, half, 0)

    for h in range(halves):
        for peer in peers:
            x_copy(h, peer, me).wait_send()
    for peer in peers:
        m_copy(peer, me).wait_send()
        p_copy(peer, me).wait_send()
    for h in range(halves):
        pltpu.make_async_copy(
            xo.at[h, pl.ds(lax.rem(me + n - 1, n) * fdev, fdev)],
            out_hbm.at[:, me, h],
            local.at[12 + halves + h],
        ).wait()
        for peer in peers:
            o_copy(h, lax.rem(peer + n - 1, n), me, peer).wait_send()
            o_copy(h, lax.rem(me + n - 1, n), peer, me).wait_recv()


HALVES = 2
BLOCKS = 1
GRANT = 40 << 20


def fused(
    latents,
    levels,
    back_reach,
    text_ids,
    text_table,
    text_proj,
    level_embed,
    step_rate,
    norm_gain,
    w_query,
    w_key,
    w_value,
    w_out,
):
    n = lax.axis_size("level")
    fdev, tokens, width = latents.shape
    pos = tokens // (n * HALVES)
    frames = fdev * n
    rows = frames * pos
    bf16, f32, i32 = jnp.bfloat16, jnp.float32, jnp.int32
    anywhere = pl.BlockSpec(memory_space=pl.ANY)
    stored = pl.BlockSpec(memory_space=pltpu.HBM)
    dma = pltpu.SemaphoreType.DMA
    block = pltpu.VMEM((HALVES, frames, pos, width), bf16)
    rolled = pltpu.VMEM((rows + fdev * pos, width), bf16)
    padded = pltpu.VMEM((rows + 2 * BAND * pos, width), bf16)
    square = pltpu.VMEM((width, width), bf16)
    out = pl.pallas_call(
        functools.partial(queue_kernel, n, BLOCKS),
        out_shape=jax.ShapeDtypeStruct((fdev, n, HALVES, pos, width), bf16),
        in_specs=[stored] * 13,
        out_specs=anywhere,
        scratch_shapes=[
            block,
            rolled,
            rolled,
            block,
            pltpu.VMEM((rows, width), bf16),
            padded,
            padded,
            padded,
            padded,
            pltpu.VMEM(text_table.shape, bf16),
            pltpu.VMEM(text_proj.shape, bf16),
            pltpu.VMEM(level_embed.shape, f32),
            pltpu.VMEM(norm_gain.shape, f32),
            square,
            square,
            square,
            square,
            pltpu.SMEM(levels.shape, i32),
            pltpu.SMEM(back_reach.shape, i32),
            pltpu.SMEM(text_ids.shape, i32),
            pltpu.SMEM(step_rate.shape, f32),
            pltpu.VMEM((n, 1, text_table.shape[1]), f32),
            pltpu.VMEM((n, 1, 128), i32),
            pltpu.VMEM((frames, 1, width), f32),
            pltpu.VMEM((frames, 1, width), f32),
            pltpu.VMEM((SPAN, frames, 1, 128), f32),
            pltpu.VMEM((width, 128), bf16),
            pltpu.VMEM((128, width), bf16),
            dma((HALVES, n)),
            dma((HALVES, n)),
            dma((n,)),
            dma((n,)),
            dma((n,)),
            dma((n,)),
            dma((HALVES, n)),
            dma((HALVES, n)),
            dma((12 + 2 * HALVES,)),
        ],
        compiler_params=pltpu.CompilerParams(
            collective_id=0, has_side_effects=True, vmem_limit_bytes=GRANT
        ),
        name="queue",
    )(
        *(
            pltpu.with_memory_space_constraint(value, pltpu.HBM)
            for value in (
                latents.reshape(fdev, n, HALVES, pos, width),
                levels,
                back_reach,
                text_ids,
                text_table,
                text_proj,
                level_embed,
                step_rate,
                norm_gain,
                w_query,
                w_key,
                w_value,
                w_out,
            )
        )
    )
    return out.reshape(fdev, tokens, width)


def general(
    latents,
    levels,
    back_reach,
    text_ids,
    text_table,
    text_proj,
    level_embed,
    step_rate,
    norm_gain,
    w_query,
    w_key,
    w_value,
    w_out,
):
    n = lax.axis_size("level")
    index = lax.axis_index("level")
    fdev, tokens, width = latents.shape
    heads = width // DH
    frames = fdev * n
    vocab = text_table.shape[0]
    spots = index * vocab + jnp.arange(vocab, dtype=jnp.int32)
    counts = jnp.sum((text_ids[:, None] == spots[None, :]).astype(jnp.float32), axis=0)
    partial = jnp.dot(
        counts.astype(jnp.bfloat16)[None, :], text_table, preferred_element_type=jnp.float32
    )
    pooled = lax.psum(partial, "level") / text_ids.shape[0]
    text_vec = jnp.dot(pooled.astype(jnp.bfloat16), text_proj, preferred_element_type=jnp.float32)
    levels = lax.all_gather(levels, "level", tiled=True)
    reach = lax.all_gather(back_reach, "level", tiled=True)
    cond = level_embed[levels] + text_vec
    rate = step_rate[levels]
    current = lax.all_to_all(latents, "level", split_axis=1, concat_axis=0, tiled=True)
    pos = tokens // n
    spot = jnp.arange(frames, dtype=jnp.int32)
    for step in range(STEPS):
        hin = current.astype(jnp.float32) + cond[:, None, :]
        power = jnp.mean(hin * hin, axis=-1, keepdims=True)
        normed = (hin * lax.rsqrt(power + 1e-06) * norm_gain).astype(jnp.bfloat16)
        flat = normed.reshape(-1, width)

        def project(weight):
            out = jnp.dot(flat, weight, preferred_element_type=jnp.float32)
            return out.astype(jnp.bfloat16).reshape(frames, pos, heads, DH).astype(jnp.float32)

        edge = ((BAND, BAND), (0, 0), (0, 0), (0, 0))
        query = project(w_query)
        keys = jnp.pad(project(w_key), edge)
        values = jnp.pad(project(w_value), edge)
        scores = []
        masks = []
        for offset in range(-BAND, BAND + 1):
            raw = jnp.sum(query * keys[BAND + offset : BAND + offset + frames], -1) / DH**0.5
            valid = (offset >= -reach) & (spot + offset >= 0) & (spot + offset < frames)
            scores.append(jnp.where(valid[:, None, None], raw, -1e30))
            masks.append(valid.astype(jnp.float32)[:, None, None])
        scores = jnp.stack(scores)
        expo = jnp.exp(scores - jnp.max(scores, axis=0)[None]) * jnp.stack(masks)
        weights = (expo / jnp.sum(expo, axis=0)[None]).astype(jnp.bfloat16).astype(jnp.float32)
        attended = jnp.zeros((frames, pos, heads, DH), jnp.float32)
        for slot in range(SPAN):
            attended = attended + weights[slot][..., None] * values[slot : slot + frames]
        noise = jnp.dot(
            attended.astype(jnp.bfloat16).reshape(-1, width),
            w_out,
            preferred_element_type=jnp.float32,
        ).reshape(frames, pos, width)
        updated = current.astype(jnp.float32) - rate[:, None, None] * noise
        current = jnp.roll(updated.astype(jnp.bfloat16), fdev, axis=0)
    return lax.all_to_all(current, "level", split_axis=0, concat_axis=1, tiled=True)


def per_device(latents, *rest):
    n = lax.axis_size("level")
    tokens = latents.shape[1]
    if tokens % (8 * HALVES * n) == 0 and latents.shape[0] % 2 == 0:
        return fused(latents, *rest)
    return general(latents, *rest)


def solution(mesh):
    in_specs = (
        P(("groups", "level"), None, None),
        P(("groups", "level")),
        P(("groups", "level")),
        P("groups"),
        P("level", None),
        P(),
        P(),
        P(),
        P(),
        P(),
        P(),
        P(),
        P(),
    )
    out_specs = P(("groups", "level"), None, None)
    return jax.shard_map(
        per_device, mesh=mesh, in_specs=in_specs, out_specs=out_specs, check_vma=False
    )
```

time: 61.8 us -> 46.2 us (0.75); the launches traced: 60.7 us -> 46.1 us
  Pallas kernels: 54.1 us -> 45.2 us
  local copies, waits for them, and re-layouts: 5.81 us -> 0.84 us
  other arithmetic: 0.75 us -> 0 us
    pallas_call x1, Pallas kernels: 54.1 us -> 45.2 us  [fused(): pl.pallas_call(functools.partial(queue_kernel, n, BLOCKS), out_shape=jax....]
    broadcast_in_dim x3 -> x0, local copies, waits for them, and re-layouts: 3.83 us -> none  [the longest x1 1.37 us: fused(): text_ids[:, None]]
    unnamed x1, local copies, waits for them, and re-layouts: 1.98 us -> 0.84 us
    convert_element_type x1 -> x0, other arithmetic: 0.75 us -> none  [fused(): meta = jnp.concatenate([levels, back_reach]).astype(f32)]
where the time goes in v2:
time: 46.2 us; the launch traced here: 46.1 us
  Pallas kernels  45.2 us (98%)
  local copies, waits for them, and re-layouts  0.84 us (2%)
    pallas_call x1, Pallas kernels, fused(): pl.pallas_call(functools.partial(queue_kernel, n, BLOCKS), out_shape=jax....  45.2 us

profile of v2, /device:TPU:25, one launch (start us, length us, event | category | flops | bytes accessed | tf_op | source)
XLA Modules:
  0.0 46.1 jit_solution(5977457944804783255)
XLA Ops:
  0.0 45.2 %queue.1 = bf16[2,16,2,8,640]{4,3,2,1,0:T(8,128)(2,1)S(1)} custom-call(bf16[2,16,2,8,640]{4,3,2,1,0:T(8,128)(2,1)} %bitcast.3, s32[2]{0:T(128)} %level_hbm.1, s32[2]{0:T(128)} %reach_hbm.1, s32[77]{0:T(128)} %ids_hbm.1, bf16[3088,1024]{1,0:T(8,128)(2,1)} %table_hbm.1, bf16[1024,640]{1,0:T(8,128)(2,1)} %proj_hbm.1, f32[16,640]{1,0:T(8,128)} %embed_hbm.1, ...), custom_call_target="tpu_custom_call" | custom-call | tf_op jit(solution)/shard_map/queue/pallas_call | solution.py:371
  45.2 0.8 %copy.15 = bf16[2,256,640]{2,1,0:T(8,128)(2,1)} copy(bf16[2,256,640]{2,1,0:T(8,128)(2,1)S(1)} %bitcast.2) | data formatting | bytes 1310720

commit v3 on v2

--- a/solution.py
+++ b/solution.py
@@ -140,9 +140,11 @@
             device_id_type=MESH,
         )
 
-    peers = [lax.rem(me + hop, n) for hop in range(1, n)]
+    order = sorted(range(1, n), key=lambda hop: min(hop, n - hop))
+    peers = [lax.rem(me + hop, n) for hop in order]
     pl.semaphore_wait(barrier, n - 1)
-    for peer in peers:
+    early = (n - 1) * 9 // 15
+    for peer in peers[:early]:
         x_copy(0, peer, me).start()
 
     stage[0].wait()
@@ -170,6 +172,8 @@
     pool[me] = partial[0:1]
     for peer in peers:
         p_copy(peer, me).start()
+    for peer in peers[early:]:
+        x_copy(0, peer, me).start()
     for h in range(1, halves):
         for peer in peers:
             x_copy(h, peer, me).start()

time: 46.2 us -> 44.4 us (0.961)
  the two profiles are of different devices: /device:TPU:25 before, /device:TPU:0 now
where the time goes in v3:
time: 44.4 us; the launch traced here: 44.3 us
  Pallas kernels  43.4 us (98%)
  local copies, waits for them, and re-layouts  0.84 us (2%)
    pallas_call x1, Pallas kernels, fused(): pl.pallas_call(functools.partial(queue_kernel, n, BLOCKS), out_shape=jax....  43.4 us

profile of v3, /device:TPU:0, one launch (start us, length us, event | category | flops | bytes accessed | tf_op | source)
XLA Modules:
  0.0 44.3 jit_solution(14287303919458992220)
XLA Ops:
  0.0 43.4 %queue.1 = bf16[2,16,2,8,640]{4,3,2,1,0:T(8,128)(2,1)S(1)} custom-call(bf16[2,16,2,8,640]{4,3,2,1,0:T(8,128)(2,1)} %bitcast.3, s32[2]{0:T(128)} %level_hbm.1, s32[2]{0:T(128)} %reach_hbm.1, s32[77]{0:T(128)} %ids_hbm.1, bf16[3088,1024]{1,0:T(8,128)(2,1)} %table_hbm.1, bf16[1024,640]{1,0:T(8,128)(2,1)} %proj_hbm.1, f32[16,640]{1,0:T(8,128)} %embed_hbm.1, ...), custom_call_target="tpu_custom_call" | custom-call | tf_op jit(solution)/shard_map/queue/pallas_call | solution.py:375
  43.4 0.8 %copy.15 = bf16[2,256,640]{2,1,0:T(8,128)(2,1)} copy(bf16[2,256,640]{2,1,0:T(8,128)(2,1)S(1)} %bitcast.2) | data formatting | bytes 1310720
